TPU v7x, 256 devices: a whole 4x4x8 slice. The times are simulated.
256 devices in a mesh: dp: 8 (over x, y_lo), fsdp: 16 (over z, core), tensor: 2 (over y_hi).
Axes of the slice: x: 4, y: 4 (y_hi: 2, y_lo: 2; y = y_hi * 2 + y_lo), z: 8, core: 2. Of those that a mesh axis runs over, the one named last changes fastest.
Arguments:
- pooled: bfloat16 [8, 3072, 1152], P('dp', 'fsdp'), may hold values from -6 to 6
- ln_gain: float32 [1152], replicated, may hold values from 0.5 to 1.5
- w_in: bfloat16 [1152, 4304], P('fsdp', 'tensor'), may hold values from -0.1875 to 0.1875
- w_out: bfloat16 [4304, 1152], P('tensor', 'fsdp'), may hold values from -0.09375 to 0.09375
- texts: bfloat16 [8, 3072, 1152], P('dp', ('fsdp', 'tensor')), may hold values from -6 to 6
Outputs:
- grad_pooled: float32 [8, 3072, 1152], P('dp', 'fsdp')
- grad_in: float32 [1152, 4304], P('fsdp', 'tensor')
- grad_out: float32 [4304, 1152], P('tensor', 'fsdp')
All inputs are finite; a program needn't handle non-finite values.
Results may differ from a plain program's by a relative error of at most 0.022.
Values may be sent and summed in bfloat16 or wider, within the bound.
A program may use at most 64 MiB of HBM per device.

v0:
```python
import jax
import jax.numpy as jnp
from jax import lax
from jax.sharding import PartitionSpec as P

ln_eps = 1e-06
norm_eps = 1e-06
logit_scale = 10.0
logit_bias = -2.0


def passed_along(block, axis, distance):
    devices = range(lax.axis_size(axis))
    route = [((i - distance) % len(devices), i) for i in devices]
    return lax.ppermute(block, axis, route)


def gelu_tanh(values):
    return jax.nn.gelu(values, approximate=True)


def unit_rows(values):
    return values / jnp.sqrt(jnp.sum(values * values, axis=-1, keepdims=True) + norm_eps)


def text_columns(first, number, block_rows, offset, stride):
    places = first + jnp.arange(number, dtype=jnp.int32)
    return places // block_rows * stride + offset + places % block_rows


def body(pooled, ln_gain, w_in, w_out, texts):
    rows = pooled[0].astype(jnp.float32)
    images = rows.shape[0]
    width = rows.shape[1]
    row_mean = jnp.mean(rows, axis=1, keepdims=True)
    centred = rows - row_mean
    inv_std = lax.rsqrt(jnp.mean(centred * centred, axis=1, keepdims=True) + ln_eps)
    normal_rows = centred * inv_std
    unit_in = (normal_rows * ln_gain).astype(jnp.bfloat16)
    full_in = lax.all_gather(w_in, "fsdp", axis=0, tiled=True)
    pre_act = jnp.dot(unit_in, full_in, preferred_element_type=jnp.float32)
    hidden = gelu_tanh(pre_act).astype(jnp.bfloat16)
    full_out = lax.all_gather(w_out, "fsdp", axis=1, tiled=True)
    partial_mix = jnp.dot(hidden, full_out, preferred_element_type=jnp.float32)
    mixed = rows + lax.psum(partial_mix.astype(jnp.bfloat16), "tensor").astype(jnp.float32)
    row_norm = jnp.sqrt(jnp.sum(mixed * mixed, axis=1, keepdims=True) + norm_eps)
    image_unit = mixed / row_norm
    image_b = image_unit.astype(jnp.bfloat16)
    text_b = unit_rows(texts[0].astype(jnp.float32)).astype(jnp.bfloat16)
    cycle_index = lax.axis_index("fsdp")
    cycle_size = lax.axis_size("fsdp")
    image_places = cycle_index * images + jnp.arange(images, dtype=jnp.int32)
    offset = lax.axis_index("tensor") * text_b.shape[0]
    block_rows = text_b.shape[0]

    def score_block(running, block, columns):
        logits = (
            logit_scale
            * jnp.einsum("rd,cd->rc", image_b, block, preferred_element_type=jnp.float32)
            + logit_bias
        )
        match = (image_places[:, None] == columns[None, :]).astype(jnp.float32)
        weights = (jax.nn.sigmoid(logits) - match).astype(jnp.bfloat16)
        return running + jnp.dot(weights, block, preferred_element_type=jnp.float32)

    def source_columns(source):
        return text_columns(source * block_rows, block_rows, block_rows, offset, images)

    empty = jnp.zeros((images, width), jnp.float32)
    running = score_block(empty, text_b, source_columns(cycle_index))

    def cycle_turn(turn, carry):
        total, moving = carry
        moving = passed_along(moving, "fsdp", 1)
        total = score_block(total, moving, source_columns((cycle_index - turn) % cycle_size))
        return (total, moving)

    running, _ = lax.fori_loop(1, cycle_size, cycle_turn, (running, text_b))
    grad_unit = logit_scale * running
    grad_unit = lax.psum(grad_unit.astype(jnp.bfloat16), "tensor").astype(jnp.float32)
    grad_mixed = (
        grad_unit - image_unit * jnp.sum(image_unit * grad_unit, axis=1, keepdims=True)
    ) / row_norm
    grad_b = grad_mixed.astype(jnp.bfloat16)
    grad_hidden = jnp.einsum("rd,fd->rf", grad_b, full_out, preferred_element_type=jnp.float32)
    _, gelu_back = jax.vjp(gelu_tanh, pre_act)
    grad_pre = gelu_back(grad_hidden)[0].astype(jnp.bfloat16)
    partial_unit = jnp.einsum("rf,df->rd", grad_pre, full_in, preferred_element_type=jnp.float32)
    grad_unit_in = lax.psum(partial_unit.astype(jnp.bfloat16), "tensor").astype(jnp.float32)
    scaled = grad_unit_in * ln_gain
    grad_rows = inv_std * (
        scaled
        - jnp.mean(scaled, axis=1, keepdims=True)
        - normal_rows * jnp.mean(scaled * normal_rows, axis=1, keepdims=True)
    )
    grad_pooled = (grad_mixed + grad_rows)[None]
    grad_in_part = lax.psum_scatter(
        jnp.einsum("rd,rf->df", unit_in, grad_pre, preferred_element_type=jnp.float32).astype(
            jnp.bfloat16
        ),
        "fsdp",
        scatter_dimension=0,
        tiled=True,
    )
    out_term = jnp.einsum("rf,rd->fd", hidden, grad_b, preferred_element_type=jnp.float32)
    grad_out_part = lax.psum_scatter(
        out_term.astype(jnp.bfloat16), "fsdp", scatter_dimension=1, tiled=True
    )
    grad_in, grad_out = (
        lax.psum(grad_in_part, "dp").astype(jnp.float32),
        lax.psum(grad_out_part, "dp").astype(jnp.float32),
    )
    return (grad_pooled, grad_in, grad_out)


def solution(mesh):
    placed = (
        P("dp", "fsdp", None),
        P(),
        P("fsdp", "tensor"),
        P("tensor", "fsdp"),
        P("dp", ("fsdp", "tensor"), None),
    )
    return jax.shard_map(
        body,
        mesh=mesh,
        in_specs=placed,
        out_specs=(P("dp", "fsdp", None), P("fsdp", "tensor"), P("tensor", "fsdp")),
        check_vma=False,
    )
```

profile of v0, /device:TPU:32, one launch (start us, length us, event | category | flops | bytes accessed | tf_op | source)
XLA Modules:
  0.0 573.5 jit_solution(10789957357336990693)
XLA Ops:
  7.2 0.7 all-gather.3.cloned.1.call-update
  8.0 0.7 all-gather.5.cloned.1.call-update
  8.8 1.1 fusion.53
  9.8 1.2 convert_reduce_fusion
  11.0 1.3 fusion.48
  12.3 42.3 %all-gather.3.cloned.1.call-done = bf16[1152,2152]{1,0:T(8,128)(2,1)} async-done(((bf16[72,2152]{1,0:T(8,128)(2,1)}), bf16[1152,2152]{1,0:T(8,128)(2,1)}) %all-gather.3.cloned.1.call-update) | async-done | bytes 4958224 | tf_op jit(solution)/shard_map/all_gather | solution.py:40
  54.6 3.8 fusion.72
  58.5 39.3 %all-gather.5.cloned.1.call-done = bf16[2152,1152]{0,1:T(8,128)(2,1)} async-done(((bf16[2152,72]{0,1:T(8,128)(2,1)}), bf16[2152,1152]{0,1:T(8,128)(2,1)}) %all-gather.5.cloned.1.call-update) | async-done | bytes 4958224 | tf_op jit(solution)/shard_map/all_gather | solution.py:43
  97.7 4.9 convolution_convert_fusion.3
  102.8 39.1 %all-reduce.8.cloned.1.call-done = bf16[192,1152]{1,0:T(8,128)(2,1)} async-done(((bf16[192,1152]{1,0:T(8,128)(2,1)}), bf16[192,1152]{1,0:T(8,128)(2,1)}) %all-reduce.8.cloned.1.call-update) | async-done | bytes 442384 | tf_op jit(solution)/shard_map/psum | solution.py:45
  142.0 1.2 multiply_reduce_fusion
  143.2 1.2 fusion.74
  145.0 101.4 %while.19 = (s32[]{:T(128)}, f32[192,1152]{1,0:T(8,128)S(1)}, bf16[96,1152]{1,0:T(8,128)(2,1)S(1)}, bf16[192,1152]{1,0:T(8,128)(2,1)S(1)}, s32[]{:T(128)}, /*ind...) while((s32[]{:T(128)}, f32[192,1152]{1,0:T(8,128)S(1)}, ...), condition=%wide.region_6.7_spmd.clone, body=%wide.region_5.6_spmd.clone.sunk | while | flops 85323472 | bytes 3762734 | solution.py:78
  145.1 5.3 collective-permute-done
  151.2 5.3 collective-permute-done
  157.3 5.3 collective-permute-done
  163.4 5.3 collective-permute-done
  169.4 5.3 collective-permute-done
  175.5 5.3 collective-permute-done
  180.8 0.7 convolution_add_fusion.2
  181.6 5.8 %collective-permute-done = bf16[96,1152]{1,0:T(8,128)(2,1)S(1)} collective-permute-done((bf16[96,1152]{1,0:T(8,128)(2,1)S(1)}, bf16[96,1152]{1,0:T(8,128)(2,1)S(1)}, u32[]{:S(2)}, u32[]{:S(2)}) %collective-permute-start) | collective-permute-done | bytes 221216 | tf_op jit(solution)/shard_map/while/body/eval_jaxpr/ppermute | solution.py:15
  188.2 6.5 %collective-permute-done = bf16[96,1152]{1,0:T(8,128)(2,1)S(1)} collective-permute-done((bf16[96,1152]{1,0:T(8,128)(2,1)S(1)}, bf16[96,1152]{1,0:T(8,128)(2,1)S(1)}, u32[]{:S(2)}, u32[]{:S(2)}) %collective-permute-start) | collective-permute-done | bytes 221216 | tf_op jit(solution)/shard_map/while/body/eval_jaxpr/ppermute | solution.py:15
  194.7 0.7 convolution_add_fusion.2
  195.5 6.5 %collective-permute-done = bf16[96,1152]{1,0:T(8,128)(2,1)S(1)} collective-permute-done((bf16[96,1152]{1,0:T(8,128)(2,1)S(1)}, bf16[96,1152]{1,0:T(8,128)(2,1)S(1)}, u32[]{:S(2)}, u32[]{:S(2)}) %collective-permute-start) | collective-permute-done | bytes 221216 | tf_op jit(solution)/shard_map/while/body/eval_jaxpr/ppermute | solution.py:15
  202.8 6.5 %collective-permute-done = bf16[96,1152]{1,0:T(8,128)(2,1)S(1)} collective-permute-done((bf16[96,1152]{1,0:T(8,128)(2,1)S(1)}, bf16[96,1152]{1,0:T(8,128)(2,1)S(1)}, u32[]{:S(2)}, u32[]{:S(2)}) %collective-permute-start) | collective-permute-done | bytes 221216 | tf_op jit(solution)/shard_map/while/body/eval_jaxpr/ppermute | solution.py:15
  209.3 0.7 convolution_add_fusion.2
  210.1 6.5 %collective-permute-done = bf16[96,1152]{1,0:T(8,128)(2,1)S(1)} collective-permute-done((bf16[96,1152]{1,0:T(8,128)(2,1)S(1)}, bf16[96,1152]{1,0:T(8,128)(2,1)S(1)}, u32[]{:S(2)}, u32[]{:S(2)}) %collective-permute-start) | collective-permute-done | bytes 221216 | tf_op jit(solution)/shard_map/while/body/eval_jaxpr/ppermute | solution.py:15
  217.4 6.5 %collective-permute-done = bf16[96,1152]{1,0:T(8,128)(2,1)S(1)} collective-permute-done((bf16[96,1152]{1,0:T(8,128)(2,1)S(1)}, bf16[96,1152]{1,0:T(8,128)(2,1)S(1)}, u32[]{:S(2)}, u32[]{:S(2)}) %collective-permute-start) | collective-permute-done | bytes 221216 | tf_op jit(solution)/shard_map/while/body/eval_jaxpr/ppermute | solution.py:15
  223.9 0.7 convolution_add_fusion.2
  224.7 6.5 %collective-permute-done = bf16[96,1152]{1,0:T(8,128)(2,1)S(1)} collective-permute-done((bf16[96,1152]{1,0:T(8,128)(2,1)S(1)}, bf16[96,1152]{1,0:T(8,128)(2,1)S(1)}, u32[]{:S(2)}, u32[]{:S(2)}) %collective-permute-start) | collective-permute-done | bytes 221216 | tf_op jit(solution)/shard_map/while/body/eval_jaxpr/ppermute | solution.py:15
  232.0 6.5 %collective-permute-done = bf16[96,1152]{1,0:T(8,128)(2,1)S(1)} collective-permute-done((bf16[96,1152]{1,0:T(8,128)(2,1)S(1)}, bf16[96,1152]{1,0:T(8,128)(2,1)S(1)}, u32[]{:S(2)}, u32[]{:S(2)}) %collective-permute-start) | collective-permute-done | bytes 221216 | tf_op jit(solution)/shard_map/while/body/eval_jaxpr/ppermute | solution.py:15
  239.3 6.5 %collective-permute-done = bf16[96,1152]{1,0:T(8,128)(2,1)S(1)} collective-permute-done((bf16[96,1152]{1,0:T(8,128)(2,1)S(1)}, bf16[96,1152]{1,0:T(8,128)(2,1)S(1)}, u32[]{:S(2)}, u32[]{:S(2)}) %collective-permute-start) | collective-permute-done | bytes 221216 | tf_op jit(solution)/shard_map/while/body/eval_jaxpr/ppermute | solution.py:15
  246.5 0.8 multiply_convert_fusion.1
  247.4 47.6 %all-reduce.10.cloned.1.call-done = bf16[192,1152]{1,0:T(8,128)(2,1)} async-done(((bf16[192,1152]{1,0:T(8,128)(2,1)}), bf16[192,1152]{1,0:T(8,128)(2,1)}) %all-reduce.10.cloned.1.call-update) | async-done | bytes 442384 | tf_op jit(solution)/shard_map/psum | solution.py:80
  294.9 1.5 fusion.49
  296.4 4.7 fusion.26
  301.2 2.4 convolution_convert_fusion.2
  303.7 3.9 convolution_convert_fusion.1
  307.9 0.8 copy-done.3
  308.6 4.1 convolution_convert_fusion
  312.8 30.4 %all-reduce.12.cloned.1.call-done = bf16[192,1152]{1,0:T(8,128)(2,1)} async-done(((bf16[192,1152]{1,0:T(8,128)(2,1)}), bf16[192,1152]{1,0:T(8,128)(2,1)}) %all-reduce.12.cloned.1.call-update) | async-done | bytes 442384 | tf_op jit(solution)/shard_map/psum | solution.py:89
  343.3 1.4 fusion.51
  344.7 64.2 %reduce-scatter.7.cloned.1.call-done = bf16[72,2152]{1,0:T(8,128)(2,1)} async-done(((bf16[1152,2152]{1,0:T(8,128)(2,1)}), bf16[72,2152]{1,0:T(8,128)(2,1)}) %reduce-scatter.7.cloned.1.call-update) | async-done | bytes 309904
  408.9 68.5 %reduce-scatter.9.cloned.1.call-done = bf16[2152,72]{0,1:T(8,128)(2,1)} async-done(((bf16[2152,1152]{0,1:T(8,128)(2,1)}), bf16[2152,72]{0,1:T(8,128)(2,1)}) %reduce-scatter.9.cloned.1.call-update) | async-done | bytes 309904
  477.4 1.5 fusion.47
  478.9 84.1 %all-reduce.14.cloned.1.call-done = (bf16[72,2152]{1,0:T(8,128)(2,1)}, bf16[2152,72]{0,1:T(8,128)(2,1)}) async-done(((bf16[72,2152]{1,0:T(8,128)(2,1)}, bf16[2152,72]{0,1:T(8,128)(2,1)}), (bf16[72,2152]{1,0:T(8,128)(2,1)}, bf16[2152,72]{0,1:T(8,128)(2,1)})) %all-reduce.14.cloned.1.call-update) | async-done | bytes 619792 | tf_op jit(solution)/shard_map/psum | solution.py:110
  563.0 1.8 convert_element_type.107
  564.9 1.8 convert_element_type.109
  (114 shorter events, 9.8 us)
Async XLA Ops:
  7.2 47.5 %copy-start = (bf16[1,192,1152]{2,1,0:T(8,128)(2,1)S(1)}, bf16[1,192,1152]{2,1,0:T(8,128)(2,1)}, u32[]{:S(2)}) copy-start(bf16[1,192,1152]{2,1,0:T(8,128)(2,1)} %param.7) | copy-start | bytes 1327108
  7.2 47.5 %copy-start.7 = (f32[1152]{0:T(1024)S(1)}, f32[1152]{0:T(1024)}, u32[]{:S(2)}) copy-start(f32[1152]{0:T(1024)} %param.8) | copy-start | bytes 13828
  7.2 47.4 %all-gather.3.cloned.1.call-start = ((), (), s32[]{:S(2)}) async-start(), calls=%async_computation.2 | async-start | bytes 5326848 | tf_op jit(solution)/shard_map/all_gather | solution.py:40
  7.9 89.8 %all-gather.5.cloned.1.call-start = ((), (), s32[]{:S(2)}) async-start(), calls=%async_computation.3 | async-start | bytes 5326848 | tf_op jit(solution)/shard_map/all_gather | solution.py:43
  8.7 133.3 %all-reduce.8.cloned.1.call-start = ((), (), s32[]{:S(2)}) async-start(), calls=%async_computation.4 | async-start | bytes 884736 | tf_op jit(solution)/shard_map/psum | solution.py:45
  58.4 44.2 %copy-start.4 = (f32[192,2152]{1,0:T(8,128)}, f32[192,2152]{1,0:T(8,128)S(1)}, u32[]{:S(2)}) copy-start(f32[192,2152]{1,0:T(8,128)S(1)} %fusion.72) | copy-start | bytes 4958212
  58.5 44.2 %copy-start.6 = (bf16[1,96,1152]{2,1,0:T(8,128)(2,1)S(1)}, bf16[1,96,1152]{2,1,0:T(8,128)(2,1)}, u32[]{:S(2)}) copy-start(bf16[1,96,1152]{2,1,0:T(8,128)(2,1)} %param.11) | copy-start | bytes 663556
  102.6 192.3 %all-reduce.10.cloned.1.call-start = ((), (), s32[]{:S(2)}) async-start(), calls=%async_computation.5 | async-start | bytes 884736 | tf_op jit(solution)/shard_map/psum | solution.py:80
  145.0 5.4 collective-permute-start
  151.1 5.4 collective-permute-start
  157.2 5.4 collective-permute-start
  163.3 5.4 collective-permute-start
  169.4 5.4 collective-permute-start
  175.4 5.4 collective-permute-start
  181.5 5.9 %collective-permute-start = (bf16[96,1152]{1,0:T(8,128)(2,1)S(1)}, bf16[96,1152]{1,0:T(8,128)(2,1)S(1)}, u32[]{:S(2)}, u32[]{:S(2)}) collective-permute-start(bf16[96,1152]{1,0:T(8,128)(2,1)S(1)} %get-tuple-element.306), channel_id=1, source_target_pairs={{30,0},{0,2},{2,4},{4,6},{6,8},{8,10},{10,12},{12,14},{14,16},{16,... | collective-permute-start | bytes 663560 | tf_op jit(solution)/shard_map/while/body/eval_jaxpr/ppermute | solution.py:15
  188.1 6.6 %collective-permute-start = (bf16[96,1152]{1,0:T(8,128)(2,1)S(1)}, bf16[96,1152]{1,0:T(8,128)(2,1)S(1)}, u32[]{:S(2)}, u32[]{:S(2)}) collective-permute-start(bf16[96,1152]{1,0:T(8,128)(2,1)S(1)} %get-tuple-element.306), channel_id=1, source_target_pairs={{30,0},{0,2},{2,4},{4,6},{6,8},{8,10},{10,12},{12,14},{14,16},{16,... | collective-permute-start | bytes 663560 | tf_op jit(solution)/shard_map/while/body/eval_jaxpr/ppermute | solution.py:15
  195.4 6.6 %collective-permute-start = (bf16[96,1152]{1,0:T(8,128)(2,1)S(1)}, bf16[96,1152]{1,0:T(8,128)(2,1)S(1)}, u32[]{:S(2)}, u32[]{:S(2)}) collective-permute-start(bf16[96,1152]{1,0:T(8,128)(2,1)S(1)} %get-tuple-element.306), channel_id=1, source_target_pairs={{30,0},{0,2},{2,4},{4,6},{6,8},{8,10},{10,12},{12,14},{14,16},{16,... | collective-permute-start | bytes 663560 | tf_op jit(solution)/shard_map/while/body/eval_jaxpr/ppermute | solution.py:15
  202.7 6.6 %collective-permute-start = (bf16[96,1152]{1,0:T(8,128)(2,1)S(1)}, bf16[96,1152]{1,0:T(8,128)(2,1)S(1)}, u32[]{:S(2)}, u32[]{:S(2)}) collective-permute-start(bf16[96,1152]{1,0:T(8,128)(2,1)S(1)} %get-tuple-element.306), channel_id=1, source_target_pairs={{30,0},{0,2},{2,4},{4,6},{6,8},{8,10},{10,12},{12,14},{14,16},{16,... | collective-permute-start | bytes 663560 | tf_op jit(solution)/shard_map/while/body/eval_jaxpr/ppermute | solution.py:15
  210.0 6.6 %collective-permute-start = (bf16[96,1152]{1,0:T(8,128)(2,1)S(1)}, bf16[96,1152]{1,0:T(8,128)(2,1)S(1)}, u32[]{:S(2)}, u32[]{:S(2)}) collective-permute-start(bf16[96,1152]{1,0:T(8,128)(2,1)S(1)} %get-tuple-element.306), channel_id=1, source_target_pairs={{30,0},{0,2},{2,4},{4,6},{6,8},{8,10},{10,12},{12,14},{14,16},{16,... | collective-permute-start | bytes 663560 | tf_op jit(solution)/shard_map/while/body/eval_jaxpr/ppermute | solution.py:15
  217.3 6.6 %collective-permute-start = (bf16[96,1152]{1,0:T(8,128)(2,1)S(1)}, bf16[96,1152]{1,0:T(8,128)(2,1)S(1)}, u32[]{:S(2)}, u32[]{:S(2)}) collective-permute-start(bf16[96,1152]{1,0:T(8,128)(2,1)S(1)} %get-tuple-element.306), channel_id=1, source_target_pairs={{30,0},{0,2},{2,4},{4,6},{6,8},{8,10},{10,12},{12,14},{14,16},{16,... | collective-permute-start | bytes 663560 | tf_op jit(solution)/shard_map/while/body/eval_jaxpr/ppermute | solution.py:15
  224.6 6.6 %collective-permute-start = (bf16[96,1152]{1,0:T(8,128)(2,1)S(1)}, bf16[96,1152]{1,0:T(8,128)(2,1)S(1)}, u32[]{:S(2)}, u32[]{:S(2)}) collective-permute-start(bf16[96,1152]{1,0:T(8,128)(2,1)S(1)} %get-tuple-element.306), channel_id=1, source_target_pairs={{30,0},{0,2},{2,4},{4,6},{6,8},{8,10},{10,12},{12,14},{14,16},{16,... | collective-permute-start | bytes 663560 | tf_op jit(solution)/shard_map/while/body/eval_jaxpr/ppermute | solution.py:15
  231.9 6.6 %collective-permute-start = (bf16[96,1152]{1,0:T(8,128)(2,1)S(1)}, bf16[96,1152]{1,0:T(8,128)(2,1)S(1)}, u32[]{:S(2)}, u32[]{:S(2)}) collective-permute-start(bf16[96,1152]{1,0:T(8,128)(2,1)S(1)} %get-tuple-element.306), channel_id=1, source_target_pairs={{30,0},{0,2},{2,4},{4,6},{6,8},{8,10},{10,12},{12,14},{14,16},{16,... | collective-permute-start | bytes 663560 | tf_op jit(solution)/shard_map/while/body/eval_jaxpr/ppermute | solution.py:15
  239.2 6.6 %collective-permute-start = (bf16[96,1152]{1,0:T(8,128)(2,1)S(1)}, bf16[96,1152]{1,0:T(8,128)(2,1)S(1)}, u32[]{:S(2)}, u32[]{:S(2)}) collective-permute-start(bf16[96,1152]{1,0:T(8,128)(2,1)S(1)} %get-tuple-element.306), channel_id=1, source_target_pairs={{30,0},{0,2},{2,4},{4,6},{6,8},{8,10},{10,12},{12,14},{14,16},{16,... | collective-permute-start | bytes 663560 | tf_op jit(solution)/shard_map/while/body/eval_jaxpr/ppermute | solution.py:15
  246.5 48.5 %copy-start.1 = (bf16[192,1152]{1,0:T(8,128)(2,1)S(1)}, bf16[192,1152]{1,0:T(8,128)(2,1)}, u32[]{:S(2)}) copy-start(bf16[192,1152]{1,0:T(8,128)(2,1)} %all-reduce.8.cloned.1.call-done) | copy-start | bytes 1327108
  246.5 49.9 %copy-start.5 = (f32[192,2152]{1,0:T(8,128)S(1)}, f32[192,2152]{1,0:T(8,128)}, u32[]{:S(2)}) copy-start(f32[192,2152]{1,0:T(8,128)} %copy-done.4) | copy-start | bytes 4958212
  247.3 95.9 %all-reduce.12.cloned.1.call-start = ((), (), s32[]{:S(2)}) async-start(), calls=%async_computation.6 | async-start | bytes 884736 | tf_op jit(solution)/shard_map/psum | solution.py:89
  294.9 6.2 %slice-start = ((s8[5013504]{0:T(1024)(128)(4,1)}), s8[4194304]{0:T(1024)(128)(4,1)S(1)}, s32[]{:S(2)}) async-start(s8[5013504]{0:T(1024)(128)(4,1)} %bitcast.75), calls=%async_computation.10 | async-start | bytes 8388608
  296.4 4.8 slice-start.1
  303.6 105.3 %reduce-scatter.7.cloned.1.call-start = ((), (), s32[]{:S(2)}) async-start(), calls=%async_computation.7 | async-start | bytes 5326848
  307.6 1.0 copy-start.3
  307.6 169.8 %reduce-scatter.9.cloned.1.call-start = ((), (), s32[]{:S(2)}) async-start(), calls=%async_computation.8 | async-start | bytes 5326848
  312.8 250.3 %all-reduce.14.cloned.1.call-start = ((), (), s32[]{:S(2)}) async-start(), calls=%async_computation.9 | async-start | bytes 1253376 | tf_op jit(solution)/shard_map/psum | solution.py:110
  343.3 134.2 %copy-start.2 = (bf16[192,1152]{1,0:T(8,128)(2,1)S(1)}, bf16[192,1152]{1,0:T(8,128)(2,1)}, u32[]{:S(2)}) copy-start(bf16[192,1152]{1,0:T(8,128)(2,1)} %all-reduce.12.cloned.1.call-done) | copy-start | bytes 1327108
Sparse Core Ops, SparseCore 0:
  9.8 44.7 all-gather.2
  56.5 41.2 all-gather.4
  102.8 39.1 all-reduce.7
  247.4 47.4 all-reduce.9
  303.7 39.4 all-reduce.11
  345.7 63.1 reduce-scatter.6
  411.5 65.8 reduce-scatter.8
  480.1 82.8 all-reduce.13
where the time goes:
time: 574 us
  waiting for transfers between devices  507 us (88%)
  matrix products  34.6 us (6%)
  other arithmetic  15.3 us (3%)
  between operations  14.3 us (2%)
    unnamed x10, waiting for transfers between devices  134 us
    ppermute x15, waiting for transfers between devices, passed_along(): return lax.ppermute(block, axis, route)  89.5 us
    psum x1, waiting for transfers between devices, body(): lax.psum(grad_in_part, 'dp').astype(jnp.float32)  84.1 us
    psum x1, waiting for transfers between devices, body(): lax.psum(grad_unit.astype(jnp.bfloat16), 'tensor').astype(jnp.float32)  47.6 us
    all_gather x1, waiting for transfers between devices, body(): full_in = lax.all_gather(w_in, 'fsdp', axis=0, tiled=True)  42.3 us
    all_gather x1, waiting for transfers between devices, body(): full_out = lax.all_gather(w_out, 'fsdp', axis=1, tiled=True)  39.3 us
    psum x1, waiting for transfers between devices, body(): lax.psum(partial_mix.astype(jnp.bfloat16), 'tensor').astype(jnp.float32)  39.1 us
    psum x1, waiting for transfers between devices, body(): lax.psum(partial_unit.astype(jnp.bfloat16), 'tensor').astype(jnp.float32)  30.4 us
  transfers between devices with their start and end apart: 23, of which 23 were waited for; matrix products, arithmetic and copies ran while one was open for 3% of the time, Pallas kernels for 0%

commit v1 on v0

--- a/solution.py
+++ b/solution.py
@@ -86,7 +86,9 @@
     _, gelu_back = jax.vjp(gelu_tanh, pre_act)
     grad_pre = gelu_back(grad_hidden)[0].astype(jnp.bfloat16)
     partial_unit = jnp.einsum("rf,df->rd", grad_pre, full_in, preferred_element_type=jnp.float32)
-    grad_unit_in = lax.psum(partial_unit.astype(jnp.bfloat16), "tensor").astype(jnp.float32)
+    grad_unit_in = jnp.sum(
+        lax.all_gather(partial_unit.astype(jnp.bfloat16), "tensor"), axis=0
+    ).astype(jnp.float32)
     scaled = grad_unit_in * ln_gain
     grad_rows = inv_std * (
         scaled

time: 574 us -> 533 us (0.929)
  waiting for transfers between devices: 507 us -> 450 us
  blocking collectives: 0 us -> 13.9 us
    psum x1 -> x0, waiting for transfers between devices: 30.4 us -> none  [body(): lax.psum(partial_unit.astype(jnp.bfloat16), 'tensor').astype(jnp.float32)]
    unnamed x10 -> x9, waiting for transfers between devices: 134 us -> 108 us
    all_gather x0 -> x1, blocking collectives: none -> 13.9 us  [body(): lax.all_gather(partial_unit.astype(jnp.bfloat16), 'tensor')]
  transfers between devices with their start and end apart: 23 -> 22, of which waited for: 23 -> 22; matrix products, arithmetic and copies ran while one was open for 3% -> 3% of each run, Pallas kernels for 0% -> 0%
where the time goes in v1:
time: 533 us
  waiting for transfers between devices  450 us (84%)
  matrix products  36.3 us (7%)
  other arithmetic  14.4 us (3%)
  between operations  14.3 us (3%)
  blocking collectives  13.9 us (3%)
    unnamed x9, waiting for transfers between devices  108 us
    ppermute x15, waiting for transfers between devices, passed_along(): return lax.ppermute(block, axis, route)  89.5 us
    psum x1, waiting for transfers between devices, body(): lax.psum(grad_in_part, 'dp').astype(jnp.float32)  84 us
    psum x1, waiting for transfers between devices, body(): lax.psum(grad_unit.astype(jnp.bfloat16), 'tensor').astype(jnp.float32)  47.6 us
    all_gather x1, waiting for transfers between devices, body(): full_in = lax.all_gather(w_in, 'fsdp', axis=0, tiled=True)  42.3 us
    all_gather x1, waiting for transfers between devices, body(): full_out = lax.all_gather(w_out, 'fsdp', axis=1, tiled=True)  39.3 us
    psum x1, waiting for transfers between devices, body(): lax.psum(partial_mix.astype(jnp.bfloat16), 'tensor').astype(jnp.float32)  39.1 us
    all_gather x1, blocking collectives, body(): lax.all_gather(partial_unit.astype(jnp.bfloat16), 'tensor')  13.9 us
  transfers between devices with their start and end apart: 22, of which 22 were waited for; matrix products, arithmetic and copies ran while one was open for 3% of the time, Pallas kernels for 0%

profile of v1, /device:TPU:32, one launch (start us, length us, event | category | flops | bytes accessed | tf_op | source)
XLA Modules:
  0.0 532.9 jit_solution(7388615795490596390)
XLA Ops:
  7.2 0.7 all-gather.4.cloned.1.call-update
  8.0 0.7 all-gather.6.cloned.1.call-update
  8.8 1.1 fusion.53
  9.8 1.2 convert_reduce_fusion
  11.0 1.3 fusion.48
  12.3 42.3 %all-gather.4.cloned.1.call-done = bf16[1152,2152]{1,0:T(8,128)(2,1)} async-done(((bf16[72,2152]{1,0:T(8,128)(2,1)}), bf16[1152,2152]{1,0:T(8,128)(2,1)}) %all-gather.4.cloned.1.call-update) | async-done | bytes 4958224 | tf_op jit(solution)/shard_map/all_gather | solution.py:40
  54.6 3.8 fusion.72
  58.5 39.3 %all-gather.6.cloned.1.call-done = bf16[2152,1152]{0,1:T(8,128)(2,1)} async-done(((bf16[2152,72]{0,1:T(8,128)(2,1)}), bf16[2152,1152]{0,1:T(8,128)(2,1)}) %all-gather.6.cloned.1.call-update) | async-done | bytes 4958224 | tf_op jit(solution)/shard_map/all_gather | solution.py:43
  97.7 4.9 convolution_convert_fusion.3
  102.8 39.1 %all-reduce.7.cloned.1.call-done = bf16[192,1152]{1,0:T(8,128)(2,1)} async-done(((bf16[192,1152]{1,0:T(8,128)(2,1)}), bf16[192,1152]{1,0:T(8,128)(2,1)}) %all-reduce.7.cloned.1.call-update) | async-done | bytes 442384 | tf_op jit(solution)/shard_map/psum | solution.py:45
  142.0 1.2 multiply_reduce_fusion
  143.2 1.2 fusion.74
  145.0 101.4 %while.19 = (s32[]{:T(128)}, f32[192,1152]{1,0:T(8,128)S(1)}, bf16[96,1152]{1,0:T(8,128)(2,1)S(1)}, bf16[192,1152]{1,0:T(8,128)(2,1)S(1)}, s32[]{:T(128)}, /*ind...) while((s32[]{:T(128)}, f32[192,1152]{1,0:T(8,128)S(1)}, ...), condition=%wide.region_6.7_spmd.clone, body=%wide.region_5.6_spmd.clone.sunk | while | flops 85323472 | bytes 3762734 | solution.py:78
  145.1 5.3 collective-permute-done
  151.2 5.3 collective-permute-done
  157.3 5.3 collective-permute-done
  163.4 5.3 collective-permute-done
  169.4 5.3 collective-permute-done
  175.5 5.3 collective-permute-done
  180.8 0.7 convolution_add_fusion.2
  181.6 5.8 %collective-permute-done = bf16[96,1152]{1,0:T(8,128)(2,1)S(1)} collective-permute-done((bf16[96,1152]{1,0:T(8,128)(2,1)S(1)}, bf16[96,1152]{1,0:T(8,128)(2,1)S(1)}, u32[]{:S(2)}, u32[]{:S(2)}) %collective-permute-start) | collective-permute-done | bytes 221216 | tf_op jit(solution)/shard_map/while/body/eval_jaxpr/ppermute | solution.py:15
  188.2 6.5 %collective-permute-done = bf16[96,1152]{1,0:T(8,128)(2,1)S(1)} collective-permute-done((bf16[96,1152]{1,0:T(8,128)(2,1)S(1)}, bf16[96,1152]{1,0:T(8,128)(2,1)S(1)}, u32[]{:S(2)}, u32[]{:S(2)}) %collective-permute-start) | collective-permute-done | bytes 221216 | tf_op jit(solution)/shard_map/while/body/eval_jaxpr/ppermute | solution.py:15
  194.7 0.7 convolution_add_fusion.2
  195.5 6.5 %collective-permute-done = bf16[96,1152]{1,0:T(8,128)(2,1)S(1)} collective-permute-done((bf16[96,1152]{1,0:T(8,128)(2,1)S(1)}, bf16[96,1152]{1,0:T(8,128)(2,1)S(1)}, u32[]{:S(2)}, u32[]{:S(2)}) %collective-permute-start) | collective-permute-done | bytes 221216 | tf_op jit(solution)/shard_map/while/body/eval_jaxpr/ppermute | solution.py:15
  202.8 6.5 %collective-permute-done = bf16[96,1152]{1,0:T(8,128)(2,1)S(1)} collective-permute-done((bf16[96,1152]{1,0:T(8,128)(2,1)S(1)}, bf16[96,1152]{1,0:T(8,128)(2,1)S(1)}, u32[]{:S(2)}, u32[]{:S(2)}) %collective-permute-start) | collective-permute-done | bytes 221216 | tf_op jit(solution)/shard_map/while/body/eval_jaxpr/ppermute | solution.py:15
  209.3 0.7 convolution_add_fusion.2
  210.1 6.5 %collective-permute-done = bf16[96,1152]{1,0:T(8,128)(2,1)S(1)} collective-permute-done((bf16[96,1152]{1,0:T(8,128)(2,1)S(1)}, bf16[96,1152]{1,0:T(8,128)(2,1)S(1)}, u32[]{:S(2)}, u32[]{:S(2)}) %collective-permute-start) | collective-permute-done | bytes 221216 | tf_op jit(solution)/shard_map/while/body/eval_jaxpr/ppermute | solution.py:15
  217.4 6.5 %collective-permute-done = bf16[96,1152]{1,0:T(8,128)(2,1)S(1)} collective-permute-done((bf16[96,1152]{1,0:T(8,128)(2,1)S(1)}, bf16[96,1152]{1,0:T(8,128)(2,1)S(1)}, u32[]{:S(2)}, u32[]{:S(2)}) %collective-permute-start) | collective-permute-done | bytes 221216 | tf_op jit(solution)/shard_map/while/body/eval_jaxpr/ppermute | solution.py:15
  223.9 0.7 convolution_add_fusion.2
  224.7 6.5 %collective-permute-done = bf16[96,1152]{1,0:T(8,128)(2,1)S(1)} collective-permute-done((bf16[96,1152]{1,0:T(8,128)(2,1)S(1)}, bf16[96,1152]{1,0:T(8,128)(2,1)S(1)}, u32[]{:S(2)}, u32[]{:S(2)}) %collective-permute-start) | collective-permute-done | bytes 221216 | tf_op jit(solution)/shard_map/while/body/eval_jaxpr/ppermute | solution.py:15
  232.0 6.5 %collective-permute-done = bf16[96,1152]{1,0:T(8,128)(2,1)S(1)} collective-permute-done((bf16[96,1152]{1,0:T(8,128)(2,1)S(1)}, bf16[96,1152]{1,0:T(8,128)(2,1)S(1)}, u32[]{:S(2)}, u32[]{:S(2)}) %collective-permute-start) | collective-permute-done | bytes 221216 | tf_op jit(solution)/shard_map/while/body/eval_jaxpr/ppermute | solution.py:15
  239.3 6.5 %collective-permute-done = bf16[96,1152]{1,0:T(8,128)(2,1)S(1)} collective-permute-done((bf16[96,1152]{1,0:T(8,128)(2,1)S(1)}, bf16[96,1152]{1,0:T(8,128)(2,1)S(1)}, u32[]{:S(2)}, u32[]{:S(2)}) %collective-permute-start) | collective-permute-done | bytes 221216 | tf_op jit(solution)/shard_map/while/body/eval_jaxpr/ppermute | solution.py:15
  246.5 0.8 multiply_convert_fusion.1
  247.4 47.6 %all-reduce.9.cloned.1.call-done = bf16[192,1152]{1,0:T(8,128)(2,1)} async-done(((bf16[192,1152]{1,0:T(8,128)(2,1)}), bf16[192,1152]{1,0:T(8,128)(2,1)}) %all-reduce.9.cloned.1.call-update) | async-done | bytes 442384 | tf_op jit(solution)/shard_map/psum | solution.py:80
  294.9 1.3 fusion.49
  296.3 4.7 fusion.26
  301.0 4.0 convolution_convert_fusion.1
  305.0 0.9 copy-done.2
  306.0 4.2 convolution_convert_fusion
  310.4 0.9 copy-done.7
  311.3 4.0 convolution_convert_fusion.2
  315.4 13.9 %all-gather = bf16[384,1152]{1,0:T(8,128)(2,1)S(1)} all-gather(bf16[192,1152]{1,0:T(8,128)(2,1)S(1)} %convolution_convert_fusion.2), channel_id=2, replica_groups=mesh['dp'=8,'fsdp'=16,'tensor'=2] {'tensor'}, dimensions={0}, use_global_device_ids=true | all-gather | bytes 1327104 | tf_op jit(solution)/shard_map/all_gather | solution.py:90
  329.9 38.7 %reduce-scatter.7.cloned.1.call-done = bf16[72,2152]{1,0:T(8,128)(2,1)} async-done(((bf16[1152,2152]{1,0:T(8,128)(2,1)}), bf16[72,2152]{1,0:T(8,128)(2,1)}) %reduce-scatter.7.cloned.1.call-update) | async-done | bytes 309904
  368.6 68.3 %reduce-scatter.9.cloned.1.call-done = bf16[2152,72]{0,1:T(8,128)(2,1)} async-done(((bf16[2152,1152]{0,1:T(8,128)(2,1)}), bf16[2152,72]{0,1:T(8,128)(2,1)}) %reduce-scatter.9.cloned.1.call-update) | async-done | bytes 309904
  436.9 1.5 fusion.47
  438.3 84.0 %all-reduce.11.cloned.1.call-done = (bf16[72,2152]{1,0:T(8,128)(2,1)}, bf16[2152,72]{0,1:T(8,128)(2,1)}) async-done(((bf16[72,2152]{1,0:T(8,128)(2,1)}, bf16[2152,72]{0,1:T(8,128)(2,1)}), (bf16[72,2152]{1,0:T(8,128)(2,1)}, bf16[2152,72]{0,1:T(8,128)(2,1)})) %all-reduce.11.cloned.1.call-update) | async-done | bytes 619792 | tf_op jit(solution)/shard_map/psum | solution.py:112
  522.4 1.8 convert_element_type.109
  524.2 1.8 convert_element_type.111
  (110 shorter events, 10.3 us)
Async XLA Ops:
  7.2 47.5 %copy-start = (bf16[1,192,1152]{2,1,0:T(8,128)(2,1)S(1)}, bf16[1,192,1152]{2,1,0:T(8,128)(2,1)}, u32[]{:S(2)}) copy-start(bf16[1,192,1152]{2,1,0:T(8,128)(2,1)} %param.7) | copy-start | bytes 1327108
  7.2 47.5 %copy-start.8 = (f32[1152]{0:T(1024)S(1)}, f32[1152]{0:T(1024)}, u32[]{:S(2)}) copy-start(f32[1152]{0:T(1024)} %param.8) | copy-start | bytes 13828
  7.2 47.4 %all-gather.4.cloned.1.call-start = ((), (), s32[]{:S(2)}) async-start(), calls=%async_computation.2 | async-start | bytes 5326848 | tf_op jit(solution)/shard_map/all_gather | solution.py:40
  7.9 89.8 %all-gather.6.cloned.1.call-start = ((), (), s32[]{:S(2)}) async-start(), calls=%async_computation.3 | async-start | bytes 5326848 | tf_op jit(solution)/shard_map/all_gather | solution.py:43
  8.7 133.3 %all-reduce.7.cloned.1.call-start = ((), (), s32[]{:S(2)}) async-start(), calls=%async_computation.4 | async-start | bytes 884736 | tf_op jit(solution)/shard_map/psum | solution.py:45
  58.4 44.2 %copy-start.3 = (f32[192,2152]{1,0:T(8,128)}, f32[192,2152]{1,0:T(8,128)S(1)}, u32[]{:S(2)}) copy-start(f32[192,2152]{1,0:T(8,128)S(1)} %fusion.72) | copy-start | bytes 4958212
  58.5 44.2 %copy-start.5 = (bf16[1,96,1152]{2,1,0:T(8,128)(2,1)S(1)}, bf16[1,96,1152]{2,1,0:T(8,128)(2,1)}, u32[]{:S(2)}) copy-start(bf16[1,96,1152]{2,1,0:T(8,128)(2,1)} %param.11) | copy-start | bytes 663556
  102.6 192.3 %all-reduce.9.cloned.1.call-start = ((), (), s32[]{:S(2)}) async-start(), calls=%async_computation.5 | async-start | bytes 884736 | tf_op jit(solution)/shard_map/psum | solution.py:80
  145.0 5.4 %collective-permute-start = (bf16[96,1152]{1,0:T(8,128)(2,1)S(1)}, bf16[96,1152]{1,0:T(8,128)(2,1)S(1)}, u32[]{:S(2)}, u32[]{:S(2)}) collective-permute-start(bf16[96,1152]{1,0:T(8,128)(2,1)S(1)} %get-tuple-element.306), channel_id=1, source_target_pairs={{30,0},{0,2},{2,4},{4,6},{6,8},{8,10},{10,12},{12,14},{14,16},{16,... | collective-permute-start | bytes 663560 | tf_op jit(solution)/shard_map/while/body/eval_jaxpr/ppermute | solution.py:15
  151.1 5.4 %collective-permute-start = (bf16[96,1152]{1,0:T(8,128)(2,1)S(1)}, bf16[96,1152]{1,0:T(8,128)(2,1)S(1)}, u32[]{:S(2)}, u32[]{:S(2)}) collective-permute-start(bf16[96,1152]{1,0:T(8,128)(2,1)S(1)} %get-tuple-element.306), channel_id=1, source_target_pairs={{30,0},{0,2},{2,4},{4,6},{6,8},{8,10},{10,12},{12,14},{14,16},{16,... | collective-permute-start | bytes 663560 | tf_op jit(solution)/shard_map/while/body/eval_jaxpr/ppermute | solution.py:15
  157.2 5.4 %collective-permute-start = (bf16[96,1152]{1,0:T(8,128)(2,1)S(1)}, bf16[96,1152]{1,0:T(8,128)(2,1)S(1)}, u32[]{:S(2)}, u32[]{:S(2)}) collective-permute-start(bf16[96,1152]{1,0:T(8,128)(2,1)S(1)} %get-tuple-element.306), channel_id=1, source_target_pairs={{30,0},{0,2},{2,4},{4,6},{6,8},{8,10},{10,12},{12,14},{14,16},{16,... | collective-permute-start | bytes 663560 | tf_op jit(solution)/shard_map/while/body/eval_jaxpr/ppermute | solution.py:15
  163.3 5.4 %collective-permute-start = (bf16[96,1152]{1,0:T(8,128)(2,1)S(1)}, bf16[96,1152]{1,0:T(8,128)(2,1)S(1)}, u32[]{:S(2)}, u32[]{:S(2)}) collective-permute-start(bf16[96,1152]{1,0:T(8,128)(2,1)S(1)} %get-tuple-element.306), channel_id=1, source_target_pairs={{30,0},{0,2},{2,4},{4,6},{6,8},{8,10},{10,12},{12,14},{14,16},{16,... | collective-permute-start | bytes 663560 | tf_op jit(solution)/shard_map/while/body/eval_jaxpr/ppermute | solution.py:15
  169.4 5.4 %collective-permute-start = (bf16[96,1152]{1,0:T(8,128)(2,1)S(1)}, bf16[96,1152]{1,0:T(8,128)(2,1)S(1)}, u32[]{:S(2)}, u32[]{:S(2)}) collective-permute-start(bf16[96,1152]{1,0:T(8,128)(2,1)S(1)} %get-tuple-element.306), channel_id=1, source_target_pairs={{30,0},{0,2},{2,4},{4,6},{6,8},{8,10},{10,12},{12,14},{14,16},{16,... | collective-permute-start | bytes 663560 | tf_op jit(solution)/shard_map/while/body/eval_jaxpr/ppermute | solution.py:15
  175.4 5.4 %collective-permute-start = (bf16[96,1152]{1,0:T(8,128)(2,1)S(1)}, bf16[96,1152]{1,0:T(8,128)(2,1)S(1)}, u32[]{:S(2)}, u32[]{:S(2)}) collective-permute-start(bf16[96,1152]{1,0:T(8,128)(2,1)S(1)} %get-tuple-element.306), channel_id=1, source_target_pairs={{30,0},{0,2},{2,4},{4,6},{6,8},{8,10},{10,12},{12,14},{14,16},{16,... | collective-permute-start | bytes 663560 | tf_op jit(solution)/shard_map/while/body/eval_jaxpr/ppermute | solution.py:15
  181.5 5.9 %collective-permute-start = (bf16[96,1152]{1,0:T(8,128)(2,1)S(1)}, bf16[96,1152]{1,0:T(8,128)(2,1)S(1)}, u32[]{:S(2)}, u32[]{:S(2)}) collective-permute-start(bf16[96,1152]{1,0:T(8,128)(2,1)S(1)} %get-tuple-element.306), channel_id=1, source_target_pairs={{30,0},{0,2},{2,4},{4,6},{6,8},{8,10},{10,12},{12,14},{14,16},{16,... | collective-permute-start | bytes 663560 | tf_op jit(solution)/shard_map/while/body/eval_jaxpr/ppermute | solution.py:15
  188.1 6.6 %collective-permute-start = (bf16[96,1152]{1,0:T(8,128)(2,1)S(1)}, bf16[96,1152]{1,0:T(8,128)(2,1)S(1)}, u32[]{:S(2)}, u32[]{:S(2)}) collective-permute-start(bf16[96,1152]{1,0:T(8,128)(2,1)S(1)} %get-tuple-element.306), channel_id=1, source_target_pairs={{30,0},{0,2},{2,4},{4,6},{6,8},{8,10},{10,12},{12,14},{14,16},{16,... | collective-permute-start | bytes 663560 | tf_op jit(solution)/shard_map/while/body/eval_jaxpr/ppermute | solution.py:15
  195.4 6.6 %collective-permute-start = (bf16[96,1152]{1,0:T(8,128)(2,1)S(1)}, bf16[96,1152]{1,0:T(8,128)(2,1)S(1)}, u32[]{:S(2)}, u32[]{:S(2)}) collective-permute-start(bf16[96,1152]{1,0:T(8,128)(2,1)S(1)} %get-tuple-element.306), channel_id=1, source_target_pairs={{30,0},{0,2},{2,4},{4,6},{6,8},{8,10},{10,12},{12,14},{14,16},{16,... | collective-permute-start | bytes 663560 | tf_op jit(solution)/shard_map/while/body/eval_jaxpr/ppermute | solution.py:15
  202.7 6.6 %collective-permute-start = (bf16[96,1152]{1,0:T(8,128)(2,1)S(1)}, bf16[96,1152]{1,0:T(8,128)(2,1)S(1)}, u32[]{:S(2)}, u32[]{:S(2)}) collective-permute-start(bf16[96,1152]{1,0:T(8,128)(2,1)S(1)} %get-tuple-element.306), channel_id=1, source_target_pairs={{30,0},{0,2},{2,4},{4,6},{6,8},{8,10},{10,12},{12,14},{14,16},{16,... | collective-permute-start | bytes 663560 | tf_op jit(solution)/shard_map/while/body/eval_jaxpr/ppermute | solution.py:15
  210.0 6.6 %collective-permute-start = (bf16[96,1152]{1,0:T(8,128)(2,1)S(1)}, bf16[96,1152]{1,0:T(8,128)(2,1)S(1)}, u32[]{:S(2)}, u32[]{:S(2)}) collective-permute-start(bf16[96,1152]{1,0:T(8,128)(2,1)S(1)} %get-tuple-element.306), channel_id=1, source_target_pairs={{30,0},{0,2},{2,4},{4,6},{6,8},{8,10},{10,12},{12,14},{14,16},{16,... | collective-permute-start | bytes 663560 | tf_op jit(solution)/shard_map/while/body/eval_jaxpr/ppermute | solution.py:15
  217.3 6.6 %collective-permute-start = (bf16[96,1152]{1,0:T(8,128)(2,1)S(1)}, bf16[96,1152]{1,0:T(8,128)(2,1)S(1)}, u32[]{:S(2)}, u32[]{:S(2)}) collective-permute-start(bf16[96,1152]{1,0:T(8,128)(2,1)S(1)} %get-tuple-element.306), channel_id=1, source_target_pairs={{30,0},{0,2},{2,4},{4,6},{6,8},{8,10},{10,12},{12,14},{14,16},{16,... | collective-permute-start | bytes 663560 | tf_op jit(solution)/shard_map/while/body/eval_jaxpr/ppermute | solution.py:15
  224.6 6.6 %collective-permute-start = (bf16[96,1152]{1,0:T(8,128)(2,1)S(1)}, bf16[96,1152]{1,0:T(8,128)(2,1)S(1)}, u32[]{:S(2)}, u32[]{:S(2)}) collective-permute-start(bf16[96,1152]{1,0:T(8,128)(2,1)S(1)} %get-tuple-element.306), channel_id=1, source_target_pairs={{30,0},{0,2},{2,4},{4,6},{6,8},{8,10},{10,12},{12,14},{14,16},{16,... | collective-permute-start | bytes 663560 | tf_op jit(solution)/shard_map/while/body/eval_jaxpr/ppermute | solution.py:15
  231.9 6.6 %collective-permute-start = (bf16[96,1152]{1,0:T(8,128)(2,1)S(1)}, bf16[96,1152]{1,0:T(8,128)(2,1)S(1)}, u32[]{:S(2)}, u32[]{:S(2)}) collective-permute-start(bf16[96,1152]{1,0:T(8,128)(2,1)S(1)} %get-tuple-element.306), channel_id=1, source_target_pairs={{30,0},{0,2},{2,4},{4,6},{6,8},{8,10},{10,12},{12,14},{14,16},{16,... | collective-permute-start | bytes 663560 | tf_op jit(solution)/shard_map/while/body/eval_jaxpr/ppermute | solution.py:15
  239.2 6.6 %collective-permute-start = (bf16[96,1152]{1,0:T(8,128)(2,1)S(1)}, bf16[96,1152]{1,0:T(8,128)(2,1)S(1)}, u32[]{:S(2)}, u32[]{:S(2)}) collective-permute-start(bf16[96,1152]{1,0:T(8,128)(2,1)S(1)} %get-tuple-element.306), channel_id=1, source_target_pairs={{30,0},{0,2},{2,4},{4,6},{6,8},{8,10},{10,12},{12,14},{14,16},{16,... | collective-permute-start | bytes 663560 | tf_op jit(solution)/shard_map/while/body/eval_jaxpr/ppermute | solution.py:15
  246.5 48.5 %copy-start.1 = (bf16[192,1152]{1,0:T(8,128)(2,1)S(1)}, bf16[192,1152]{1,0:T(8,128)(2,1)}, u32[]{:S(2)}) copy-start(bf16[192,1152]{1,0:T(8,128)(2,1)} %all-reduce.7.cloned.1.call-done) | copy-start | bytes 1327108
  246.5 49.8 %copy-start.4 = (f32[192,2152]{1,0:T(8,128)S(1)}, f32[192,2152]{1,0:T(8,128)}, u32[]{:S(2)}) copy-start(f32[192,2152]{1,0:T(8,128)} %copy-done.3) | copy-start | bytes 4958212
  247.3 121.2 %reduce-scatter.7.cloned.1.call-start = ((), (), s32[]{:S(2)}) async-start(), calls=%async_computation.6 | async-start | bytes 5326848
  300.9 4.0 copy-start.6
  305.0 1.0 copy-start.2
  305.0 131.8 %reduce-scatter.9.cloned.1.call-start = ((), (), s32[]{:S(2)}) async-start(), calls=%async_computation.7 | async-start | bytes 5326848
  310.2 1.1 copy-start.7
  310.2 212.1 %all-reduce.11.cloned.1.call-start = ((), (), s32[]{:S(2)}) async-start(), calls=%async_computation.8 | async-start | bytes 1253376 | tf_op jit(solution)/shard_map/psum | solution.py:112
Sparse Core Ops, SparseCore 0:
  9.8 44.7 all-gather.3
  56.5 41.2 all-gather.5
  102.8 39.1 all-reduce.6
  247.4 47.4 all-reduce.8
  305.1 63.3 reduce-scatter.6
  371.0 65.8 reduce-scatter.8
  439.6 82.7 all-reduce.10
